TPU v7x, 512 devices: a whole 4x4x16 slice. The times are simulated.
512 devices in a mesh: col: 64 (over y, z), row: 8 (over x, core).
Axes of the slice: x: 4, y: 4, z: 16, core: 2. Of those that a mesh axis runs over, the one named last changes fastest.
Arguments:
- x_block: bfloat16 [8, 8192, 64], P('row', 'col'), may hold values from -6 to 6
- tiles: bfloat16 [64, 8, 96, 128, 128], P('col', 'row'), may hold values from -0.078125 to 0.078125
- tile_rows: int32 [64, 8, 96], P('col', 'row'), may hold values from 0 to 63
- tile_cols: int32 [64, 8, 96], P('col', 'row'), may hold values from 0 to 7
- tile_count: int32 [64, 8], P('col', 'row'), may hold values from 1 to 96, as said below
Outputs:
- filtered: bfloat16 [8, 8192, 64], P('row', 'col')
- gram: float32 [64, 64], replicated
Inputs may be any that keep to these rules, and one draw needn't show every extreme that they name: `tile_count`: padding slots hold arbitrary tiles and indices; every draw has some device with all 96 slots live.
All inputs are finite; a program needn't handle non-finite values.
Results may differ from a plain program's by a relative error of at most 0.0049.
Values may be sent and summed in bfloat16 or wider, within the bound.
A program may use at most 64 MiB of HBM per device.

v0:
```python
import jax
import jax.numpy as jnp
from jax import lax
from jax.sharding import PartitionSpec as P


def local(x_block, tiles, tile_rows, tile_cols, tile_count):
    n_col = lax.axis_size("col")
    n_row = lax.axis_size("row")
    tile_data = tiles[0, 0]
    rows_here = tile_rows[0, 0]
    cols_here = tile_cols[0, 0]
    count_here = tile_count[0, 0]
    vectors = x_block.shape[2]
    slots = tile_data.shape[0]
    live = jnp.arange(slots, dtype=jnp.int32) < count_here
    placing = (
        (rows_here[None, :] == jnp.arange(n_col, dtype=jnp.int32)[:, None]) & live[None, :]
    ).astype(jnp.float32)

    def apply_local(segment):
        slab_vecs = lax.all_gather(segment[0], "row", axis=0, tiled=True)
        picked = slab_vecs.reshape(n_row, 128, vectors)[cols_here]
        products = jnp.einsum("tij,tjk->tik", tile_data, picked, preferred_element_type=jnp.float32)
        products = products.reshape(slots, 128 * vectors)
        band_sums = jnp.dot(placing, products, precision=lax.Precision.HIGH)
        owned = lax.psum_scatter(band_sums, "col", scatter_dimension=0, tiled=True)
        return owned.reshape(1, 128, vectors)

    first = apply_local(x_block).astype(jnp.bfloat16)
    second = apply_local(first)
    gram_term = jnp.dot(first[0].astype(jnp.float32).T, second[0], precision=lax.Precision.HIGHEST)
    gram = lax.psum(gram_term, ("col", "row")) / (n_col * n_row * 128)
    return (second.astype(jnp.bfloat16), gram)


def solution(mesh):
    placed = (
        P("row", "col", None),
        P("col", "row", None, None, None),
        P("col", "row", None),
        P("col", "row", None),
        P("col", "row"),
    )
    return jax.shard_map(
        local, mesh=mesh, in_specs=placed, out_specs=(P("row", "col", None), P()), check_vma=False
    )
```

profile of v0, /device:TPU:1, one launch (start us, length us, event | category | flops | bytes accessed | tf_op | source)
XLA Modules:
  0.0 760.7 jit_solution(15123610081769181831)
XLA Ops:
  7.2 0.0 copy-start
  7.2 0.0 all-reduce.5.cloned.1.call-start
  8.0 0.7 fusion.20
  8.8 18.2 %all-gather = bf16[1,1024,64]{1,2,0:T(8,128)(2,1)S(1)} all-gather(bf16[1,128,64]{1,2,0:T(8,128)(2,1)} %param.5), channel_id=2, replica_groups=mesh['col'=64,'row'=8] {'row'}, dimensions={1}, use_global_device_ids=true | all-gather | bytes 147456 | tf_op jit(solution)/shard_map/all_gather | solution.py:22
  27.1 2.0 gather_fusion
  29.0 0.0 copy-done
  29.0 5.3 fusion.4
  34.4 0.0 copy-start.3
  34.4 5.1 copy.18
  39.4 0.0 copy-done.3
  39.4 5.1 fusion.14
  44.5 250.4 %all-reduce.6 = bf16[64,8192]{1,0:T(8,128)(2,1)} all-reduce(f32[64,8192]{1,0:T(8,128)} %fusion.14), channel_id=3, replica_groups=mesh['col'=64,'row'=8] {'col'}, use_global_device_ids=true, to_apply=%region_0.0.clone | all-reduce | flops 524288 | bytes 3145728
  294.9 1.3 dynamic-slice
  296.2 1.7 fusion.10
  297.9 0.1 convert_element_type.27
  298.0 0.0 copy-start.1
  298.0 66.5 %all_gather.7 = bf16[1024,64]{1,0:T(8,128)(2,1)S(1)} all-gather(bf16[128,64]{1,0:T(8,128)(2,1)S(1)} %convert_element_type.27), channel_id=1, replica_groups=mesh['col'=64,'row'=8] {'row'}, dimensions={0}, use_global_device_ids=true | all-gather | bytes 147456 | tf_op jit(solution)/shard_map/all_gather | solution.py:22
  364.5 0.0 copy-done.1
  364.5 0.1 copy.20
  364.6 2.0 gather_fusion.1
  366.6 5.3 fusion.7
  371.9 5.1 copy.21
  377.0 0.0 copy-start.2
  377.0 5.1 fusion.12
  382.0 0.0 all-reduce.5.cloned.1.call-update
  382.1 257.0 %all-reduce.5.cloned.1.call-done = f32[64,8192]{1,0:T(8,128)} async-done(((f32[64,8192]{1,0:T(8,128)}), f32[64,8192]{1,0:T(8,128)}) %all-reduce.5.cloned.1.call-update) | async-done | bytes 2097168
  639.1 1.7 convert_reduce_fusion
  640.8 0.1 convert_element_type.29
  640.9 0.7 copy.22
  641.6 1.7 dynamic-slice_reduce_fusion
  643.3 0.1 squeeze_reshape.3
  643.4 0.0 copy-done.2
  643.4 0.2 fusion.21
  643.6 109.7 %psum.7 = f32[64,64]{1,0:T(8,128)S(1)} all-reduce(f32[64,64]{1,0:T(8,128)S(1)} %fusion.21), channel_id=1, replica_groups=mesh['col'=64,'row'=8] {'col','row'}, use_global_device_ids=true, to_apply=%region_2.0 | all-reduce | flops 4096 | bytes 32768 | tf_op jit(solution)/shard_map/psum | solution.py:33
  753.3 0.6 broadcast_multiply_fusion
  (4 shorter events, 0.1 us)
Async XLA Ops:
  7.2 21.8 %copy-start = (bf16[1,1,96,128,128]{4,3,2,1,0:T(8,128)(2,1)S(1)}, bf16[1,1,96,128,128]{4,3,2,1,0:T(8,128)(2,1)}, u32[]{:S(2)}) copy-start(bf16[1,1,96,128,128]{4,3,2,1,0:T(8,128)(2,1)} %param.6) | copy-start | bytes 9437188
  7.2 631.9 %all-reduce.5.cloned.1.call-start = ((), (), s32[]{:S(2)}) async-start(), calls=%async_computation | async-start | bytes 4194304
  34.4 5.1 copy-start.3
  298.0 66.5 %copy-start.1 = (bf16[128,64]{1,0:T(8,128)(2,1)}, bf16[128,64]{1,0:T(8,128)(2,1)S(1)}, u32[]{:S(2)}) copy-start(bf16[128,64]{1,0:T(8,128)(2,1)S(1)} %convert_element_type.27) | copy-start | bytes 49156
  377.0 266.4 %copy-start.2 = (bf16[128,64]{1,0:T(8,128)(2,1)S(1)}, bf16[128,64]{1,0:T(8,128)(2,1)}, u32[]{:S(2)}) copy-start(bf16[128,64]{1,0:T(8,128)(2,1)} %copy-done.1) | copy-start | bytes 49156
Sparse Core Ops, SparseCore 0:
  382.2 256.8 all-reduce.4
where the time goes:
time: 761 us
  blocking collectives  445 us (58%)
  waiting for transfers between devices  257 us (34%)
  local copies, waits for them, and re-layouts  21.7 us (3%)
  matrix products  21 us (3%)
  between operations  14.9 us (2%)
    unnamed x2, waiting for transfers between devices  257 us
    unnamed x1, blocking collectives  250 us
    psum x1, blocking collectives, local(): gram = lax.psum(gram_term, ('col', 'row')) / (n_col * n_row * 128)  110 us
    all_gather x2, blocking collectives, apply_local(): slab_vecs = lax.all_gather(segment[0], 'row', axis=0, tiled=True)  84.7 us
  transfers between devices with their start and end apart: 1, of which 1 were waited for; matrix products, arithmetic and copies ran while one was open for 0% of the time, Pallas kernels for 0%

commit v1 on v0

v1 whole, which is shorter than its diff:
```python
import functools

import jax
import jax.numpy as jnp
from jax import lax
from jax.experimental import pallas as pl
from jax.experimental.pallas import tpu as pltpu
from jax.sharding import PartitionSpec as P

MESH = pl.DeviceIdType.MESH
F32 = jnp.float32
BF16 = jnp.bfloat16
NY, NZ, NROW = 4, 16, 8
SLOTS = 96
CHUNKS = 2
PER = NZ // CHUNKS
HALF = PER // 2
OFFSETS = [8 + ((j + 1) // 2) * (1 if j % 2 == 0 else -1) for j in range(NZ)]
A_SIDE, B_SIDE = 0, 1


def encode(p):
    return (p * jnp.abs(p)).astype(BF16)


def decode(u):
    u = u.astype(F32)
    return u * lax.rsqrt(jnp.maximum(jnp.abs(u), 1e-37))


def rows_to_lanes(a, b):
    i = lax.broadcasted_iota(jnp.int32, (64, 128), 0)
    j = lax.broadcasted_iota(jnp.int32, (64, 128), 1)
    left = jnp.where(i == j, 1.0, 0.0).astype(BF16)
    right = jnp.where(i + 64 == j, 1.0, 0.0).astype(BF16)
    out = jnp.dot(a, left, preferred_element_type=F32)
    return out + jnp.dot(b, right, preferred_element_type=F32)


def kernel(
    table, x_ref, tiles_ref, filtered_ref, gram_ref,
    tile_buf, slab, wide, seg,
    y_far, y_near, y_relay, r_far, r_near, r_relay, z_out, z_in,
    g_send, g_row, g_y, g_z, g_all,
    tile_sem, ag_send, ag_recv, y_send, y_recv, z_send, z_recv, g_ssem, g_rsem,
):
    col, row = lax.axis_index("col"), lax.axis_index("row")
    y, z = lax.div(col, NZ), lax.rem(col, NZ)

    def at_row(step):
        return (col, lax.rem(row + step, NROW))

    def at_y(step):
        return (lax.rem(y + step, NY) * NZ + z, row)

    def at_z(step):
        return (y * NZ + lax.rem(z + step, NZ), row)

    def remote(src, dst, send, recv, device):
        return pltpu.make_async_remote_copy(
            src_ref=src, dst_ref=dst, send_sem=send, recv_sem=recv, device_id=device, device_id_type=MESH
        )

    tile_copy = pltpu.make_async_copy(tiles_ref, tile_buf, tile_sem)
    tile_copy.start()

    barrier = pltpu.get_barrier_semaphore()
    peers = [at_row(i) for i in range(1, NROW)] + [at_y(i) for i in range(1, NY)] + [at_z(i) for i in range(1, NZ)]
    for peer in peers:
        pl.semaphore_signal(barrier, inc=1, device_id=peer, device_id_type=MESH)
    own_x = rows_to_lanes(x_ref[0, 0:64, :], x_ref[0, 64:128, :]).astype(BF16)
    slab[0, row] = own_x
    seg[SLOTS] = jnp.zeros((64, 128), F32)
    pl.semaphore_wait(barrier, len(peers))

    lane = lax.broadcasted_iota(jnp.int32, (64, 128), 1)
    sent = []

    def gather(k):
        for i in range(1, NROW):
            c = remote(slab.at[k, row], slab.at[k, row], ag_send.at[k, i], ag_recv.at[k, i], at_row(i))
            c.start()
            sent.append(c)
        for i in range(1, NROW):
            source = lax.rem(row + NROW - i, NROW)
            remote(
                slab.at[k, source], slab.at[k, source], ag_send.at[k, i], ag_recv.at[k, i], at_row(i)
            ).wait_recv()

    def products(k):
        def widen(r, _):
            here = slab[k, r].astype(F32)
            there = pltpu.roll(here, 64, 1)
            low = lane < 64
            zero = jnp.zeros_like(here)
            wide[r, 0:64, :] = jnp.where(low, here, zero).astype(BF16)
            wide[r, 64:128, :] = jnp.where(low, there, zero).astype(BF16)
            wide[r, 128:192, :] = jnp.where(low, zero, there).astype(BF16)
            wide[r, 192:256, :] = jnp.where(low, zero, here).astype(BF16)
            return 0

        lax.fori_loop(0, NROW, widen, 0)

        group = 8

        def step(i, acc):
            base = i * group
            done = []
            for j in range(group):
                slot = table[0, base + j]
                tile = jnp.concatenate([tile_buf[slot, 0:64, :], tile_buf[slot, 64:128, :]], axis=1)
                done.append(jnp.dot(tile, wide[table[1, base + j]], preferred_element_type=F32))
            for j in range(group):
                acc = acc * table[2, base + j].astype(F32) + done[j]
                seg[base + j] = acc
            return acc

        lax.fori_loop(0, SLOTS // group, step, jnp.zeros((64, 128), F32))

    def partial(y_step, offset):
        block = lax.rem(y + y_step, NY) * NZ + lax.rem(z + offset, NZ)
        return seg[table[3, block]]

    def reduce_scatter(k):
        groups = [[OFFSETS[q * PER + h * HALF : q * PER + (h + 1) * HALF] for h in range(2)] for q in range(CHUNKS)]
        ways = {A_SIDE: (1, NY - 1), B_SIDE: (NY - 1, 1)}
        copies = {}
        for q in range(CHUNKS):
            for h in (A_SIDE, B_SIDE):
                for j, offset in enumerate(groups[q][h]):
                    y_far[k, q, h, j] = encode(partial(2, offset))
                c = remote(
                    y_far.at[k, q, h], r_far.at[k, q, h], y_send.at[k, q, h, 0], y_recv.at[k, q, h, 0], at_y(ways[h][0])
                )
                c.start()
                copies[q, h, 0] = c
        for q in range(CHUNKS):
            for h in (A_SIDE, B_SIDE):
                for j, offset in enumerate(groups[q][h]):
                    y_near[k, q, h, j] = encode(partial(ways[h][1], offset))
                c = remote(
                    y_near.at[k, q, h], r_near.at[k, q, h], y_send.at[k, q, h, 1], y_recv.at[k, q, h, 1], at_y(ways[h][1])
                )
                c.start()
                copies[q, h, 1] = c
            for h in (A_SIDE, B_SIDE):
                copies[q, h, 0].wait_recv()
                for j, offset in enumerate(groups[q][h]):
                    y_relay[k, q, h, j] = encode(partial(ways[h][0], offset) + decode(r_far[k, q, h, j]))
                c = remote(
                    y_relay.at[k, q, h], r_relay.at[k, q, h], y_send.at[k, q, h, 2], y_recv.at[k, q, h, 2], at_y(ways[h][0])
                )
                c.start()
                copies[q, h, 2] = c
        own = None
        for q in range(CHUNKS):
            for h in (A_SIDE, B_SIDE):
                copies[q, h, 1].wait_recv()
                copies[q, h, 2].wait_recv()
                for j, offset in enumerate(groups[q][h]):
                    total = partial(0, offset) + decode(r_near[k, q, h, j]) + decode(r_relay[k, q, h, j])
                    if offset == 0:
                        own = total
                        continue
                    z_out[k, offset] = encode(total)
                    c = remote(
                        z_out.at[k, offset], z_in.at[k, offset], z_send.at[k, offset], z_recv.at[k, offset], at_z(offset)
                    )
                    c.start()
                    copies["z", offset] = c
        for offset in OFFSETS[::-1][1:]:
            copies["z", offset].wait_recv()
            own = own + decode(z_in[k, offset])
        sent.extend(copies.values())
        return own

    gather(0)
    tile_copy.wait()
    products(0)
    first = reduce_scatter(0).astype(BF16)
    slab[1, row] = first
    gather(1)
    products(1)
    second = reduce_scatter(1)

    filtered_ref[0, 0:64, :] = second[:, 0:64].astype(BF16)
    filtered_ref[0, 64:128, :] = pltpu.roll(second, 64, 1)[:, 0:64].astype(BF16)

    turned = first.astype(F32).T.astype(BF16)
    high = second.astype(BF16)
    rest = second - high.astype(F32)
    mid = rest.astype(BF16)
    low = (rest - mid.astype(F32)).astype(BF16)
    both = jnp.dot(turned, low, preferred_element_type=F32)
    both = both + jnp.dot(turned, mid, preferred_element_type=F32)
    both = both + jnp.dot(turned, high, preferred_element_type=F32)
    term = both[0:64, :] + pltpu.roll(both[64:128, :], 64, 1)
    lane32 = lax.broadcasted_iota(jnp.int32, (32, 128), 1)
    packed = jnp.where(lane32 < 64, term[0:32, :], pltpu.roll(term[32:64, :], 64, 1))
    for r in range(NROW):
        g_send[r] = packed[4 * r : 4 * r + 4, :]

    def spread(buf, size, mine, device, sem, source=None):
        for i in range(1, size):
            src = buf.at[mine] if source is None else source(i)
            c = remote(src, buf.at[mine], g_ssem.at[sem + i], g_rsem.at[sem + i], device(i))
            c.start()
            sent.append(c)
        for i in range(1, size):
            other = buf.at[lax.rem(mine + size - i, size)]
            remote(other, other, g_ssem.at[sem + i], g_rsem.at[sem + i], device(i)).wait_recv()

    def added(buf, size):
        total = buf[0]
        for i in range(1, size):
            total = total + buf[i]
        return total

    g_row[row] = g_send[row]
    spread(g_row, NROW, row, at_row, 0, lambda i: g_send.at[lax.rem(row + i, NROW)])
    g_y[y] = added(g_row, NROW)
    spread(g_y, NY, y, at_y, 8)
    g_z[z] = added(g_y, NY)
    spread(g_z, NZ, z, at_z, 16)
    g_all[row] = added(g_z, NZ) * (1.0 / (NROW * NY * NZ * 128))
    spread(g_all, NROW, row, at_row, 32)
    for r in range(NROW):
        piece = g_all[r]
        gram_ref[4 * r : 4 * r + 4, :] = piece[:, 0:64]
        gram_ref[32 + 4 * r : 36 + 4 * r, :] = pltpu.roll(piece, 64, 1)[:, 0:64]
    for c in sent:
        c.wait_send()


def tables(rows, cols, count):
    slot = jnp.arange(SLOTS, dtype=jnp.int32)
    key = jnp.where(slot < count, rows, 64)
    before = (key[None, :] < key[:, None]) | ((key[None, :] == key[:, None]) & (slot[None, :] < slot[:, None]))
    rank = before.astype(jnp.int32).sum(1)
    seen = ((key[None, :] == key[:, None]) & (slot[None, :] < slot[:, None])).any(1).astype(jnp.int32)
    packed = slot + SLOTS * (jnp.clip(cols, 0, NROW - 1) + NROW * seen)
    ordered = jnp.where(rank[None, :] == slot[:, None], packed[None, :], 0).sum(1)
    block = jnp.arange(64, dtype=jnp.int32)
    upto = (key[None, :] <= block[:, None]).astype(jnp.int32).sum(1)
    any_here = (key[None, :] == block[:, None]).any(1)
    last = jnp.where(any_here, upto - 1, SLOTS)
    lines = [ordered % SLOTS, (ordered // SLOTS) % NROW, ordered // (SLOTS * NROW), jnp.pad(last, (0, SLOTS - 64))]
    return jnp.stack(lines).astype(jnp.int32)


def local(x_block, tiles, tile_rows, tile_cols, tile_count):
    table = tables(tile_rows[0, 0], tile_cols[0, 0], tile_count[0, 0])
    dma = pltpu.SemaphoreType.DMA
    vmem = pl.BlockSpec(memory_space=pltpu.VMEM)
    filtered, gram = pl.pallas_call(
        kernel,
        out_shape=(jax.ShapeDtypeStruct((1, 128, 64), BF16), jax.ShapeDtypeStruct((64, 64), F32)),
        in_specs=[pl.BlockSpec(memory_space=pltpu.SMEM), vmem, pl.BlockSpec(memory_space=pl.ANY)],
        out_specs=(vmem, vmem),
        scratch_shapes=[
            pltpu.VMEM((SLOTS, 128, 128), BF16),
            pltpu.VMEM((2, NROW, 64, 128), BF16),
            pltpu.VMEM((NROW, 256, 128), BF16),
            pltpu.VMEM((SLOTS + 1, 64, 128), F32),
            *[pltpu.VMEM((2, CHUNKS, 2, HALF, 64, 128), BF16) for _ in range(6)],
            pltpu.VMEM((2, NZ, 64, 128), BF16),
            pltpu.VMEM((2, NZ, 64, 128), BF16),
            pltpu.VMEM((NROW, 4, 128), F32),
            pltpu.VMEM((NROW, 4, 128), F32),
            pltpu.VMEM((NY, 4, 128), F32),
            pltpu.VMEM((NZ, 4, 128), F32),
            pltpu.VMEM((NROW, 4, 128), F32),
            dma,
            dma((2, NROW)),
            dma((2, NROW)),
            dma((2, CHUNKS, 2, 3)),
            dma((2, CHUNKS, 2, 3)),
            dma((2, NZ)),
            dma((2, NZ)),
            dma((40,)),
            dma((40,)),
        ],
        compiler_params=pltpu.CompilerParams(
            collective_id=0, has_side_effects=True, vmem_limit_bytes=40 * 1024 * 1024
        ),
    )(table, x_block, tiles.reshape(SLOTS, 128, 128))
    return filtered, gram


def solution(mesh):
    placed = (
        P("row", "col", None),
        P("col", "row", None, None, None),
        P("col", "row", None),
        P("col", "row", None),
        P("col", "row"),
    )
    return jax.shard_map(
        local, mesh=mesh, in_specs=placed, out_specs=(P("row", "col", None), P()), check_vma=False
    )
```

time: 761 us -> 103 us (0.14)
  blocking collectives: 445 us -> 0 us
  waiting for transfers between devices: 257 us -> 0 us
  Pallas kernels: 0 us -> 95.3 us
  matrix products: 21 us -> 0 us
  local copies, waits for them, and re-layouts: 21.7 us -> 4.03 us
  between operations: 14.9 us -> 1.34 us
    unnamed x2 -> x0, waiting for transfers between devices: 257 us -> none
    unnamed x1 -> x0, blocking collectives: 250 us -> none
    psum x1 -> x0, blocking collectives: 110 us -> none  [local(): gram = lax.psum(gram_term, ('col', 'row')) / (n_col * n_row * 128)]
    pallas_call x0 -> x1, Pallas kernels: none -> 95.3 us  [local(): pl.pallas_call(kernel, out_shape=(jax.ShapeDtypeStruct((1, 128, 64), BF16...]
    all_gather x2 -> x0, blocking collectives: 84.7 us -> none  [apply_local(): slab_vecs = lax.all_gather(segment[0], 'row', axis=0, tiled=True)]
    dot_general x5 -> x0, matrix products: 21 us -> none  [the longest x2 10.7 us: apply_local(): jnp.einsum('tij,tjk->tik', tile_data, picked, preferred_element_type=jnp....]
    dot_general x2 -> x0, local copies, waits for them, and re-layouts: 10.1 us -> none  [apply_local(): jnp.einsum('tij,tjk->tik', tile_data, picked, preferred_element_type=jnp....]
  transfers between devices with their start and end apart: 1 -> 0, of which waited for: 1 -> 0; matrix products, arithmetic and copies ran while one was open for 0% -> 0% of each run, Pallas kernels for 0% -> 0%
where the time goes in v1:
time: 103 us
  Pallas kernels  95.3 us (93%)
  local copies, waits for them, and re-layouts  4.03 us (4%)
  other arithmetic  2.06 us (2%)
  between operations  1.34 us (1%)
    pallas_call x1, Pallas kernels, local(): pl.pallas_call(kernel, out_shape=(jax.ShapeDtypeStruct((1, 128, 64), BF16...  95.3 us
    unnamed x4, local copies, waits for them, and re-layouts  3.33 us

profile of v1, /device:TPU:1, one launch (start us, length us, event | category | flops | bytes accessed | tf_op | source)
XLA Modules:
  0.0 102.7 jit_solution(13158453595939793133)
XLA Ops:
  1.3 0.7 compare_select_fusion.2
  1.9 0.1 convert_reduce_fusion.1
  2.0 0.1 fusion.2
  2.2 0.2 fusion.1
  2.4 0.2 convert_reduce_fusion
  2.6 0.7 fusion.7
  3.2 0.1 select_reduce_fusion
  3.4 0.8 copy.9.x_ref
  4.2 0.0 copy-start
  4.2 1.9 %copy-done = bf16[1,1,96,128,128]{4,3,2,1,0:T(8,128)(2,1)S(1)} copy-done((bf16[1,1,96,128,128]{4,3,2,1,0:T(8,128)(2,1)S(1)}, bf16[1,1,96,128,128]{4,3,2,1,0:T(8,128)(2,1)}, u32[]{:S(2)}) %copy-start) | copy-done | bytes 3145752
  6.1 95.3 %shard_map.68 = (bf16[1,128,64]{2,1,0:T(8,128)(2,1)S(1)}, f32[64,64]{1,0:T(8,128)S(1)}) custom-call(s32[4,96]{1,0:T(4,128)S(1)} %pad_add_fusion.table, bf16[1,128,64]{2,1,0:T(8,128)(2,1)S(1)} %copy.9.x_ref, bf16[96,128,128]{2,1,0:T(8,128)(2,1)S(1)} %bitcast.35), custom_call_target="tpu_custom_call" | custom-call | tf_op jit(solution)/shard_map/pallas_call | solution.py:255
  101.4 0.7 copy.10
  102.1 0.6 copy.13
  (4 shorter events, 0.0 us)
Async XLA Ops:
  4.2 1.9 %copy-start = (bf16[1,1,96,128,128]{4,3,2,1,0:T(8,128)(2,1)S(1)}, bf16[1,1,96,128,128]{4,3,2,1,0:T(8,128)(2,1)}, u32[]{:S(2)}) copy-start(bf16[1,1,96,128,128]{4,3,2,1,0:T(8,128)(2,1)} %param.6) | copy-start | bytes 9437188

commit v2 on v1

v2 whole, which is shorter than its diff:
```python
import functools

import jax
import jax.numpy as jnp
from jax import lax
from jax.experimental import pallas as pl
from jax.experimental.pallas import tpu as pltpu
from jax.sharding import PartitionSpec as P

MESH = pl.DeviceIdType.MESH
F32 = jnp.float32
BF16 = jnp.bfloat16
NY, NZ, NROW = 4, 16, 8
SLOTS = 96
CHUNKS = 4
PER = NZ // CHUNKS
OFFSETS = [8 + ((j + 1) // 2) * (1 if j % 2 == 0 else -1) for j in range(NZ)]
Y_STEPS = (2, 1, 3)
NT = (((1,), (1,)), ((), ()))


def encode(p):
    return (p * jnp.abs(p)).astype(BF16)


def decode(u):
    u = u.astype(F32)
    return u * lax.rsqrt(jnp.maximum(jnp.abs(u), 1e-37))


def kernel(
    table, x_ref, tiles_ref, filtered_ref, gram_ref,
    tile_buf, slab_x, slab_first, seg, y_out, y_in, z_out, z_in, first_z,
    g_send, g_row, g_y, g_z, g_all,
    in_sem, ag_send, ag_recv, y_send, y_recv, z_send, z_recv, f_send, f_recv, g_ssem, g_rsem,
):
    col, row = lax.axis_index("col"), lax.axis_index("row")
    y, z = lax.div(col, NZ), lax.rem(col, NZ)

    def at_row(step):
        return (col, lax.rem(row + step, NROW))

    def at_y(step):
        return (lax.rem(y + step, NY) * NZ + z, row)

    def at_z(step):
        return (y * NZ + lax.rem(z + step, NZ), row)

    def remote(src, dst, send, recv, device):
        return pltpu.make_async_remote_copy(
            src_ref=src, dst_ref=dst, send_sem=send, recv_sem=recv, device_id=device, device_id_type=MESH
        )

    x_copy = pltpu.make_async_copy(x_ref.at[0], slab_x.at[row], in_sem.at[0])
    x_copy.start()
    tile_copy = pltpu.make_async_copy(tiles_ref, tile_buf, in_sem.at[1])
    tile_copy.start()

    barrier = pltpu.get_barrier_semaphore()
    z_steps = OFFSETS[:-1]
    row_steps = (4, 5, 3, 2, 6, 7, 1)
    peers = [at_z(i) for i in z_steps] + [at_y(i) for i in Y_STEPS] + [at_row(i) for i in row_steps]
    for peer in peers:
        pl.semaphore_signal(barrier, inc=1, device_id=peer, device_id_type=MESH)
    seg[SLOTS] = jnp.zeros((64, 128), F32)
    x_copy.wait()
    pl.semaphore_wait(barrier, len(peers))

    sent = []
    slabs = (slab_x, slab_first)

    def gather_start(k):
        for i in row_steps:
            c = remote(slabs[k].at[row], slabs[k].at[row], ag_send.at[k, i], ag_recv.at[k, i], at_row(i))
            c.start()
            sent.append(c)

    def gather_wait(k):
        for i in row_steps:
            here = slabs[k].at[lax.rem(row + NROW - i, NROW)]
            remote(here, here, ag_send.at[k, i], ag_recv.at[k, i], at_row(i)).wait_recv()

    def products(k):
        group = 8

        def step(i, acc):
            base = i * group
            done = [
                lax.dot_general(
                    slabs[k][table[1, base + j]], tile_buf[table[0, base + j]], NT, preferred_element_type=F32
                )
                for j in range(group)
            ]
            for j in range(group):
                acc = acc * table[2, base + j].astype(F32) + done[j]
                seg[base + j] = acc
            return acc

        lax.fori_loop(0, SLOTS // group, step, jnp.zeros((64, 128), F32))

    def partial(y_step, offset):
        block = lax.rem(y + y_step, NY) * NZ + lax.rem(z + offset, NZ)
        return seg[table[3, block]]

    def scatter_start(k, seen):
        for q in range(CHUNKS):
            offsets = OFFSETS[q * PER : (q + 1) * PER]
            for s in Y_STEPS:
                for j, offset in enumerate(offsets):
                    y_out[k, q, s, j] = encode(partial(s, offset))
                c = remote(y_out.at[k, q, s], y_in.at[k, q, s], y_send.at[k, q, s], y_recv.at[k, q, s], at_y(s))
                c.start()
                sent.append(c)
        own = None
        for q in range(CHUNKS):
            offsets = OFFSETS[q * PER : (q + 1) * PER]
            for s in Y_STEPS:
                remote(
                    y_out.at[k, q, s], y_in.at[k, q, s], y_send.at[k, q, s], y_recv.at[k, q, s], at_y(s)
                ).wait_recv()
            sums = []
            for j, offset in enumerate(offsets):
                total = partial(0, offset)
                for s in Y_STEPS:
                    total = total + decode(y_in[k, q, s, j])
                sums.append(total)
                if offset == 0:
                    own = total
                    continue
                z_out[k, offset] = encode(total)
                c = remote(
                    z_out.at[k, offset], z_in.at[k, offset], z_send.at[k, offset], z_recv.at[k, offset], at_z(offset)
                )
                c.start()
                sent.append(c)
            seen(offsets, sums)
        return own

    def scatter_wait(k, own):
        for offset in z_steps[::-1]:
            here = z_in.at[k, offset]
            remote(z_out.at[k, offset], here, z_send.at[k, offset], z_recv.at[k, offset], at_z(offset)).wait_recv()
            own = own + decode(here[...])
        return own

    gather_start(0)
    tile_copy.wait()
    gather_wait(0)
    products(0)
    first = scatter_wait(0, scatter_start(0, lambda offsets, sums: None)).astype(BF16)
    slab_first[row] = first
    gather_start(1)
    first_z[0] = first
    for i in z_steps:
        c = remote(slab_first.at[row], first_z.at[NZ - i], f_send.at[i], f_recv.at[i], at_z(i))
        c.start()
        sent.append(c)
    gather_wait(1)
    products(1)

    terms = []

    def gram_terms(offsets, sums):
        if not terms:
            for i in z_steps:
                here = first_z.at[NZ - i]
                remote(slab_first.at[row], here, f_send.at[i], f_recv.at[i], at_z(i)).wait_recv()
        left = jnp.concatenate([first_z[offset] for offset in offsets], axis=1)
        right = jnp.concatenate(sums, axis=1)
        high = right.astype(BF16)
        rest = (right - high.astype(F32)).astype(BF16)
        term = lax.dot_general(left, rest, NT, preferred_element_type=F32)
        terms.append(term + lax.dot_general(left, high, NT, preferred_element_type=F32))

    own = scatter_start(1, gram_terms)
    term = terms[0]
    for t in terms[1:]:
        term = term + t
    for r in range(NROW):
        g_send[r] = term[8 * r : 8 * r + 8, :]

    def spread(buf, steps, size, mine, device, sem, source=None):
        for i in steps:
            src = buf.at[mine] if source is None else source(i)
            c = remote(src, buf.at[mine], g_ssem.at[sem + i], g_rsem.at[sem + i], device(i))
            c.start()
            sent.append(c)

        def wait():
            for i in steps:
                other = buf.at[lax.rem(mine + size - i, size)]
                remote(other, other, g_ssem.at[sem + i], g_rsem.at[sem + i], device(i)).wait_recv()

        return wait

    def added(buf, size):
        total = buf[0]
        for i in range(1, size):
            total = total + buf[i]
        return total

    g_row[row] = g_send[row]
    spread(g_row, row_steps, NROW, row, at_row, 0, lambda i: g_send.at[lax.rem(row + i, NROW)])()
    g_y[y] = added(g_row, NROW)
    spread(g_y, Y_STEPS, NY, y, at_y, 8)()
    g_z[z] = added(g_y, NY)
    z_wait = spread(g_z, z_steps, NZ, z, at_z, 16)
    filtered_ref[0] = scatter_wait(1, own).astype(BF16)
    z_wait()
    g_all[row] = added(g_z, NZ) * (1.0 / (NROW * NY * NZ * 128))
    spread(g_all, row_steps, NROW, row, at_row, 32)()
    for r in range(NROW):
        gram_ref[8 * r : 8 * r + 8, :] = g_all[r]
    for c in sent:
        c.wait_send()


def tables(rows, cols, count):
    slot = jnp.arange(SLOTS, dtype=jnp.int32)
    key = jnp.where(slot < count, rows, 64)
    before = (key[None, :] < key[:, None]) | ((key[None, :] == key[:, None]) & (slot[None, :] < slot[:, None]))
    rank = before.astype(jnp.int32).sum(1)
    seen = ((key[None, :] == key[:, None]) & (slot[None, :] < slot[:, None])).any(1).astype(jnp.int32)
    packed = slot + SLOTS * (jnp.clip(cols, 0, NROW - 1) + NROW * seen)
    ordered = jnp.where(rank[None, :] == slot[:, None], packed[None, :], 0).sum(1)
    block = jnp.arange(64, dtype=jnp.int32)
    upto = (key[None, :] <= block[:, None]).astype(jnp.int32).sum(1)
    any_here = (key[None, :] == block[:, None]).any(1)
    last = jnp.where(any_here, upto - 1, SLOTS)
    lines = [ordered % SLOTS, (ordered // SLOTS) % NROW, ordered // (SLOTS * NROW), jnp.pad(last, (0, SLOTS - 64))]
    return jnp.stack(lines).astype(jnp.int32)


def local(x_block, tiles, tile_rows, tile_cols, tile_count):
    table = tables(tile_rows[0, 0], tile_cols[0, 0], tile_count[0, 0])
    dma = pltpu.SemaphoreType.DMA
    vmem = pl.BlockSpec(memory_space=pltpu.VMEM)
    hbm = pl.BlockSpec(memory_space=pl.ANY)
    filtered, gram = pl.pallas_call(
        kernel,
        out_shape=(jax.ShapeDtypeStruct((1, 64, 128), BF16), jax.ShapeDtypeStruct((64, 64), F32)),
        in_specs=[pl.BlockSpec(memory_space=pltpu.SMEM), hbm, hbm],
        out_specs=(vmem, vmem),
        scratch_shapes=[
            pltpu.VMEM((SLOTS, 128, 128), BF16),
            pltpu.VMEM((NROW, 64, 128), BF16),
            pltpu.VMEM((NROW, 64, 128), BF16),
            pltpu.VMEM((SLOTS + 1, 64, 128), F32),
            pltpu.VMEM((2, CHUNKS, NY, PER, 64, 128), BF16),
            pltpu.VMEM((2, CHUNKS, NY, PER, 64, 128), BF16),
            pltpu.VMEM((2, NZ, 64, 128), BF16),
            pltpu.VMEM((2, NZ, 64, 128), BF16),
            pltpu.VMEM((NZ, 64, 128), BF16),
            pltpu.VMEM((NROW, 8, 64), F32),
            pltpu.VMEM((NROW, 8, 64), F32),
            pltpu.VMEM((NY, 8, 64), F32),
            pltpu.VMEM((NZ, 8, 64), F32),
            pltpu.VMEM((NROW, 8, 64), F32),
            dma((2,)),
            dma((2, NROW)),
            dma((2, NROW)),
            dma((2, CHUNKS, NY)),
            dma((2, CHUNKS, NY)),
            dma((2, NZ)),
            dma((2, NZ)),
            dma((NZ,)),
            dma((NZ,)),
            dma((40,)),
            dma((40,)),
        ],
        compiler_params=pltpu.CompilerParams(
            collective_id=0, has_side_effects=True, vmem_limit_bytes=60 * 1024 * 1024
        ),
    )(table, jnp.swapaxes(x_block, 1, 2), tiles.reshape(SLOTS, 128, 128))
    return jnp.swapaxes(filtered, 1, 2), gram


def solution(mesh):
    placed = (
        P("row", "col", None),
        P("col", "row", None, None, None),
        P("col", "row", None),
        P("col", "row", None),
        P("col", "row"),
    )
    return jax.shard_map(
        local, mesh=mesh, in_specs=placed, out_specs=(P("row", "col", None), P()), check_vma=False
    )
```

time: 103 us -> 92.8 us (0.901)
  Pallas kernels: 95.3 us -> 85.8 us
  local copies, waits for them, and re-layouts: 4.03 us -> 2.7 us
    pallas_call x1, Pallas kernels: 95.3 us -> 85.8 us  [local(): pl.pallas_call(kernel, out_shape=(jax.ShapeDtypeStruct((1, 64, 128), BF16...]
    unnamed x4 -> x2, local copies, waits for them, and re-layouts: 3.33 us -> 2.7 us
where the time goes in v2:
time: 92.8 us; the launch traced here: 92.5 us
  Pallas kernels  85.8 us (92%)
  local copies, waits for them, and re-layouts  2.7 us (3%)
  other arithmetic  2.63 us (3%)
  between operations  1.33 us (1%)
    pallas_call x1, Pallas kernels, local(): pl.pallas_call(kernel, out_shape=(jax.ShapeDtypeStruct((1, 64, 128), BF16...  85.8 us
    unnamed x2, local copies, waits for them, and re-layouts  2.7 us

profile of v2, /device:TPU:1, one launch (start us, length us, event | category | flops | bytes accessed | tf_op | source)
XLA Modules:
  0.0 92.5 jit_solution(3875113334839717490)
XLA Ops:
  1.3 0.7 compare_select_fusion.2
  1.9 0.1 convert_reduce_fusion.1
  2.0 0.1 fusion.2
  2.2 0.2 fusion.1
  2.4 0.2 convert_reduce_fusion
  2.6 0.7 fusion.7
  3.2 0.1 select_reduce_fusion
  3.4 0.6 pad_add_fusion.table
  4.0 85.8 %shard_map.68 = (bf16[1,64,128]{2,1,0:T(8,128)(2,1)}, f32[64,64]{1,0:T(8,128)}) custom-call(s32[4,96]{1,0:T(4,128)} %pad_add_fusion.table, bf16[1,64,128]{2,1,0:T(8,128)(2,1)} %bitcast.38, bf16[96,128,128]{2,1,0:T(8,128)(2,1)} %bitcast.37), custom_call_target="tpu_custom_call" | custom-call | tf_op jit(solution)/shard_map/pallas_call | solution.py:239
  89.8 1.3 %copy.10 = bf16[1,128,64]{1,2,0:T(8,128)(2,1)} copy(bf16[1,128,64]{1,2,0:T(8,128)(2,1)} %bitcast.39) | data formatting | bytes 32768
  91.1 1.4 %copy.11 = f32[64,64]{1,0:T(8,128)} copy(f32[64,64]{1,0:T(8,128)} %get-tuple-element.12) | data formatting | bytes 32768
  (3 shorter events, 0.0 us)

commit v3 on v0

v3 whole, which is shorter than its diff:
```python
import functools

import jax
import jax.numpy as jnp
from jax import lax
from jax.experimental import pallas as pl
from jax.experimental.pallas import tpu as pltpu
from jax.sharding import PartitionSpec as P

MESH = pl.DeviceIdType.MESH
F32 = jnp.float32
BF16 = jnp.bfloat16
NY, NZ, NROW = 4, 16, 8
SLOTS = 96
PARTS = 2
WIDE = 64 // PARTS
CHUNKS = 2
PER = NZ // CHUNKS
OFFSETS = [8 + ((j + 1) // 2) * (1 if j % 2 == 0 else -1) for j in range(NZ)]
Y_STEPS = (2, 1, 3)
NT = (((1,), (1,)), ((), ()))


def encode(p):
    return (p * jnp.abs(p)).astype(BF16)


def decode(u):
    u = u.astype(F32)
    return u * lax.rsqrt(jnp.maximum(jnp.abs(u), 1e-37))


def kernel(
    x_ref, tiles_ref, rows_ref, cols_ref, count_ref, filtered_ref, gram_ref,
    tile_buf, rows_buf, cols_buf, lines, table, slab_x0, slab_x1, slab_f0, slab_f1, seg,
    y_out, y_in, z_out, z_in, first_z, g_send, g_row, g_y, g_z, g_all,
    in_sem, ag_send, ag_recv, y_send, y_recv, z_send, z_recv, f_send, f_recv, g_ssem, g_rsem,
):
    col, row = lax.axis_index("col"), lax.axis_index("row")
    y, z = lax.div(col, NZ), lax.rem(col, NZ)

    def at_row(step):
        return (col, lax.rem(row + step, NROW))

    def at_y(step):
        return (lax.rem(y + step, NY) * NZ + z, row)

    def at_z(step):
        return (y * NZ + lax.rem(z + step, NZ), row)

    def remote(src, dst, send, recv, device):
        return pltpu.make_async_remote_copy(
            src_ref=src, dst_ref=dst, send_sem=send, recv_sem=recv, device_id=device, device_id_type=MESH
        )

    slabs = ((slab_x0, slab_x1), (slab_f0, slab_f1))
    inward = [
        pltpu.make_async_copy(rows_ref, rows_buf, in_sem.at[0]),
        pltpu.make_async_copy(cols_ref, cols_buf, in_sem.at[1]),
        *[
            pltpu.make_async_copy(x_ref.at[0, p * WIDE : (p + 1) * WIDE], slabs[0][p].at[row], in_sem.at[3 + p])
            for p in range(PARTS)
        ],
    ]
    for c in inward:
        c.start()
    barrier = pltpu.get_barrier_semaphore()
    z_steps = OFFSETS[:-1]
    row_steps = (4, 5, 3, 2, 6, 7, 1)
    peers = [at_z(i) for i in z_steps] + [at_y(i) for i in Y_STEPS] + [at_row(i) for i in row_steps]
    for peer in peers:
        pl.semaphore_signal(barrier, inc=1, device_id=peer, device_id_type=MESH)
    for p in range(PARTS):
        seg[p, SLOTS] = jnp.zeros((WIDE, 128), F32)
    tile_copy = pltpu.make_async_copy(tiles_ref, tile_buf, in_sem.at[5])
    tile_copy.start()
    for c in inward:
        c.wait()
    lines[...] = tables(rows_buf[...], cols_buf[...], count_ref[0, 0])
    table_copy = pltpu.make_async_copy(lines, table, in_sem.at[6])
    table_copy.start()
    pl.semaphore_wait(barrier, len(peers))

    sent = []

    def waiting(send, recv, ref):
        return remote(ref, ref, send, recv, at_row(1))

    def gather_start(k, p):
        for i in row_steps:
            here = slabs[k][p].at[row]
            remote(here, here, ag_send.at[k, p], ag_recv.at[k, p], at_row(i)).start()
        sent.append(waiting(ag_send.at[k, p], ag_recv.at[k, p], slabs[k][p].at[: NROW - 1]))

    def gather_wait(k, p):
        waiting(ag_send.at[k, p], ag_recv.at[k, p], slabs[k][p].at[: NROW - 1]).wait_recv()

    def products(k, p):
        group = 8

        def step(i, acc):
            base = i * group
            done = [
                lax.dot_general(
                    slabs[k][p][table[1, base + j]], tile_buf[table[0, base + j]], NT, preferred_element_type=F32
                )
                for j in range(group)
            ]
            for j in range(group):
                acc = acc * table[2, base + j].astype(F32) + done[j]
                seg[p, base + j] = acc
            return acc

        lax.fori_loop(0, SLOTS // group, step, jnp.zeros((WIDE, 128), F32))

    def partial(p, y_step, offset):
        block = lax.rem(y + y_step, NY) * NZ + lax.rem(z + offset, NZ)
        return seg[p, table[3, block]]

    def y_start(k, p):
        for q in range(CHUNKS):
            for n, s in enumerate(Y_STEPS):
                for j, offset in enumerate(OFFSETS[q * PER : (q + 1) * PER]):
                    y_out[k, p, q, n, j] = encode(partial(p, s, offset))
                remote(
                    y_out.at[k, p, q, n], y_in.at[k, p, q, n], y_send.at[k, p], y_recv.at[k, p, q], at_y(s)
                ).start()
        sent.append(waiting(y_send.at[k, p], y_recv.at[k, p, 0], y_out.at[k, p]))

    def z_start(k, p, q):
        offsets = OFFSETS[q * PER : (q + 1) * PER]
        waiting(y_send.at[k, p], y_recv.at[k, p, q], y_in.at[k, p, q]).wait_recv()
        sums = []
        for j, offset in enumerate(offsets):
            total = partial(p, 0, offset)
            for n in range(NY - 1):
                total = total + decode(y_in[k, p, q, n, j])
            sums.append(total)
            if offset:
                at = offset - 1
                z_out[k, p, at] = encode(total)
                remote(z_out.at[k, p, at], z_in.at[k, p, at], z_send.at[k, p], z_recv.at[k, p], at_z(offset)).start()
        if q == CHUNKS - 1:
            sent.append(waiting(z_send.at[k, p], z_recv.at[k, p], z_out.at[k, p]))
        return offsets, sums

    def z_wait(k, p, own):
        waiting(z_send.at[k, p], z_recv.at[k, p], z_in.at[k, p]).wait_recv()
        for at in range(NZ - 1):
            own = own + decode(z_in[k, p, at])
        return own

    for p in range(PARTS):
        gather_start(0, p)
    tile_copy.wait()
    table_copy.wait()
    for p in range(PARTS):
        gather_wait(0, p)
        products(0, p)
        y_start(0, p)
    own = []
    for p in range(PARTS):
        for q in range(CHUNKS):
            _, sums = z_start(0, p, q)
        own.append(sums[-1])

    for p in range(PARTS):
        first = z_wait(0, p, own[p]).astype(BF16)
        slabs[1][p][row] = first
        gather_start(1, p)
        first_z[p, 0] = first
        for i in z_steps:
            remote(slabs[1][p].at[row], first_z.at[p, NZ - i], f_send.at[p], f_recv.at[p], at_z(i)).start()
        sent.append(waiting(f_send.at[p], f_recv.at[p], first_z.at[p, 1:]))
    for p in range(PARTS):
        gather_wait(1, p)
        products(1, p)
        y_start(1, p)
    for p in range(PARTS):
        waiting(f_send.at[p], f_recv.at[p], first_z.at[p, 1:]).wait_recv()

    own = []
    for p in range(PARTS):
        term = None
        for q in range(CHUNKS):
            offsets, sums = z_start(1, p, q)
            left = jnp.concatenate(
                [jnp.concatenate([first_z[h, offset] for offset in offsets], axis=1) for h in range(PARTS)], axis=0
            )
            right = jnp.concatenate(sums, axis=1)
            high = right.astype(BF16)
            rest = (right - high.astype(F32)).astype(BF16)
            here = lax.dot_general(rest, left, NT, preferred_element_type=F32)
            here = here + lax.dot_general(high, left, NT, preferred_element_type=F32)
            term = here if term is None else term + here
        own.append(sums[-1])
        for r in range(NROW // PARTS):
            g_send[p * (NROW // PARTS) + r] = term[8 * r : 8 * r + 8, :]

    def spread(buf, steps, size, mine, device, sem, source=None):
        for i in steps:
            src = buf.at[mine] if source is None else source(i)
            remote(src, buf.at[mine], g_ssem.at[sem], g_rsem.at[sem], device(i)).start()
        both = waiting(g_ssem.at[sem], g_rsem.at[sem], buf.at[: size - 1])
        sent.append(both)
        return both.wait_recv

    def added(buf, size):
        total = buf[0]
        for i in range(1, size):
            total = total + buf[i]
        return total

    g_row[row] = g_send[row]
    spread(g_row, row_steps, NROW, row, at_row, 0, lambda i: g_send.at[lax.rem(row + i, NROW)])()
    g_y[y] = added(g_row, NROW)
    spread(g_y, Y_STEPS, NY, y, at_y, 1)()
    g_z[z] = added(g_y, NY)
    g_wait = spread(g_z, z_steps, NZ, z, at_z, 2)
    for p in range(PARTS):
        filtered_ref[0, p * WIDE : (p + 1) * WIDE, :] = z_wait(1, p, own[p]).astype(BF16)
    g_wait()
    g_all[row] = added(g_z, NZ) * (1.0 / (NROW * NY * NZ * 128))
    spread(g_all, row_steps, NROW, row, at_row, 3)()
    gram_ref[...] = jnp.concatenate([g_all[r] for r in range(NROW)], axis=0).T
    for c in sent:
        c.wait_send()


def tables(rows, cols, count):
    size = (SLOTS, SLOTS)
    across = lax.broadcasted_iota(jnp.int32, size, 1)
    down = lax.broadcasted_iota(jnp.int32, size, 0)

    def turned(line):
        return jnp.where(across == down, line, 0).sum(1, keepdims=True)

    key = jnp.where(across[0:1] < count, rows, 64)
    key_down = turned(key)
    equal = (key == key_down) & (across < down)
    rank = jnp.where((key < key_down) | equal, 1, 0).sum(1, keepdims=True)
    seen = jnp.where(equal, 1, 0).max(1, keepdims=True)
    packed = down[:, 0:1] + 128 * (turned(cols & (NROW - 1)) + NROW * seen)
    ordered = jnp.where(rank == across, packed, 0).sum(0, keepdims=True)
    upto = jnp.where(key_down <= across, 1, 0).sum(0, keepdims=True)
    here = jnp.where(key_down == across, 1, 0).sum(0, keepdims=True)
    last = jnp.where(here > 0, upto - 1, SLOTS)
    return jnp.concatenate([ordered & 127, (ordered >> 7) & (NROW - 1), ordered >> 10, last], axis=0)


def local(x_block, tiles, tile_rows, tile_cols, tile_count):
    dma = pltpu.SemaphoreType.DMA
    vmem = pl.BlockSpec(memory_space=pltpu.VMEM)
    filtered, gram = pl.pallas_call(
        kernel,
        out_shape=(jax.ShapeDtypeStruct((1, 64, 128), BF16), jax.ShapeDtypeStruct((64, 64), F32)),
        in_specs=[pl.BlockSpec(memory_space=pltpu.HBM)] * 4 + [pl.BlockSpec(memory_space=pltpu.SMEM)],
        out_specs=(vmem, vmem),
        scratch_shapes=[
            pltpu.VMEM((SLOTS, 128, 128), BF16),
            pltpu.VMEM((1, SLOTS), jnp.int32),
            pltpu.VMEM((1, SLOTS), jnp.int32),
            pltpu.VMEM((4, SLOTS), jnp.int32),
            pltpu.SMEM((4, SLOTS), jnp.int32),
            *[pltpu.VMEM((NROW, WIDE, 128), BF16) for _ in range(2 * PARTS)],
            pltpu.VMEM((PARTS, SLOTS + 1, WIDE, 128), F32),
            pltpu.VMEM((2, PARTS, CHUNKS, NY - 1, PER, WIDE, 128), BF16),
            pltpu.VMEM((2, PARTS, CHUNKS, NY - 1, PER, WIDE, 128), BF16),
            pltpu.VMEM((2, PARTS, NZ - 1, WIDE, 128), BF16),
            pltpu.VMEM((2, PARTS, NZ - 1, WIDE, 128), BF16),
            pltpu.VMEM((PARTS, NZ, WIDE, 128), BF16),
            pltpu.VMEM((NROW, 8, 64), F32),
            pltpu.VMEM((NROW, 8, 64), F32),
            pltpu.VMEM((NY, 8, 64), F32),
            pltpu.VMEM((NZ, 8, 64), F32),
            pltpu.VMEM((NROW, 8, 64), F32),
            dma((7,)),
            *[dma((2, PARTS))] * 3,
            dma((2, PARTS, CHUNKS)),
            *[dma((2, PARTS))] * 2,
            *[dma((PARTS,))] * 2,
            *[dma((4,))] * 2,
        ],
        compiler_params=pltpu.CompilerParams(
            collective_id=0, has_side_effects=True, vmem_limit_bytes=52 * 1024 * 1024
        ),
    )(*[pltpu.with_memory_space_constraint(a, pltpu.HBM) for a in (
        jnp.swapaxes(x_block, 1, 2), tiles.reshape(SLOTS, 128, 128), tile_rows.reshape(1, SLOTS),
        tile_cols.reshape(1, SLOTS),
    )], tile_count)
    return jnp.swapaxes(filtered, 1, 2), gram


def solution(mesh):
    placed = (
        P("row", "col", None),
        P("col", "row", None, None, None),
        P("col", "row", None),
        P("col", "row", None),
        P("col", "row"),
    )
    return jax.shard_map(
        local, mesh=mesh, in_specs=placed, out_specs=(P("row", "col", None), P()), check_vma=False
    )
```

time: 761 us -> 80.5 us (0.11)
  blocking collectives: 445 us -> 0 us
  waiting for transfers between devices: 257 us -> 0 us
  Pallas kernels: 0 us -> 77.9 us
  matrix products: 21 us -> 0 us
  local copies, waits for them, and re-layouts: 21.7 us -> 1.22 us
  between operations: 14.9 us -> 1.29 us
    unnamed x2 -> x0, waiting for transfers between devices: 257 us -> none
    unnamed x1 -> x0, blocking collectives: 250 us -> none
    psum x1 -> x0, blocking collectives: 110 us -> none  [local(): gram = lax.psum(gram_term, ('col', 'row')) / (n_col * n_row * 128)]
    all_gather x2 -> x0, blocking collectives: 84.7 us -> none  [apply_local(): slab_vecs = lax.all_gather(segment[0], 'row', axis=0, tiled=True)]
    pallas_call x0 -> x1, Pallas kernels: none -> 77.9 us  [local(): pl.pallas_call(kernel, out_shape=(jax.ShapeDtypeStruct((1, 64, 128), BF16...]
    dot_general x5 -> x0, matrix products: 21 us -> none  [the longest x2 10.7 us: apply_local(): jnp.einsum('tij,tjk->tik', tile_data, picked, preferred_element_type=jnp....]
    dot_general x2 -> x0, local copies, waits for them, and re-layouts: 10.1 us -> none  [apply_local(): jnp.einsum('tij,tjk->tik', tile_data, picked, preferred_element_type=jnp....]
  transfers between devices with their start and end apart: 1 -> 0, of which waited for: 1 -> 0; matrix products, arithmetic and copies ran while one was open for 0% -> 0% of each run, Pallas kernels for 0% -> 0%
where the time goes in v3:
time: 80.5 us; the launch traced here: 80.4 us
  Pallas kernels  77.9 us (97%)
  between operations  1.29 us (2%)
  local copies, waits for them, and re-layouts  1.22 us (2%)
    pallas_call x1, Pallas kernels, local(): pl.pallas_call(kernel, out_shape=(jax.ShapeDtypeStruct((1, 64, 128), BF16...  77.9 us

profile of v3, /device:TPU:1, one launch (start us, length us, event | category | flops | bytes accessed | tf_op | source)
XLA Modules:
  0.0 80.4 jit_solution(986305414707160890)
XLA Ops:
  1.3 77.9 %shard_map.68 = (bf16[1,64,128]{2,1,0:T(8,128)(2,1)S(1)}, f32[64,64]{1,0:T(8,128)S(1)}) custom-call(bf16[1,64,128]{2,1,0:T(8,128)(2,1)} %bitcast.7, bf16[96,128,128]{2,1,0:T(8,128)(2,1)} %bitcast.6, s32[1,96]{1,0:T(1,128)} %bitcast.8, s32[1,96]{1,0:T(1,128)} %bitcast.9, s32[1,1]{1,0:T(1,128)S(6)} %copy.9.count_ref), custom_call_target="tpu_custom_call" | custom-call | tf_op jit(solution)/shard_map/pallas_call | solution.py:254
  79.1 0.6 copy.10
  79.7 0.6 copy.11

commit v4 on v3

--- a/solution.py
+++ b/solution.py
@@ -14,7 +14,7 @@
 SLOTS = 96
 PARTS = 2
 WIDE = 64 // PARTS
-CHUNKS = 2
+CHUNKS = 4
 PER = NZ // CHUNKS
 OFFSETS = [8 + ((j + 1) // 2) * (1 if j % 2 == 0 else -1) for j in range(NZ)]
 Y_STEPS = (2, 1, 3)
@@ -96,7 +96,7 @@
         waiting(ag_send.at[k, p], ag_recv.at[k, p], slabs[k][p].at[: NROW - 1]).wait_recv()
 
     def products(k, p):
-        group = 8
+        group = 32
 
         def step(i, acc):
             base = i * group
@@ -176,14 +176,15 @@
         gather_wait(1, p)
         products(1, p)
         y_start(1, p)
-    for p in range(PARTS):
-        waiting(f_send.at[p], f_recv.at[p], first_z.at[p, 1:]).wait_recv()
 
     own = []
     for p in range(PARTS):
         term = None
         for q in range(CHUNKS):
             offsets, sums = z_start(1, p, q)
+            if p == q == 0:
+                for h in range(PARTS):
+                    waiting(f_send.at[h], f_recv.at[h], first_z.at[h, 1:]).wait_recv()
             left = jnp.concatenate(
                 [jnp.concatenate([first_z[h, offset] for offset in offsets], axis=1) for h in range(PARTS)], axis=0
             )

time: 80.5 us -> 76.8 us (0.954)
  Pallas kernels: 77.9 us -> 74.2 us
    pallas_call x1, Pallas kernels: 77.9 us -> 74.2 us  [local(): pl.pallas_call(kernel, out_shape=(jax.ShapeDtypeStruct((1, 64, 128), BF16...]
where the time goes in v4:
time: 76.8 us; the launch traced here: 76.7 us
  Pallas kernels  74.2 us (97%)
  between operations  1.29 us (2%)
  local copies, waits for them, and re-layouts  1.22 us (2%)
    pallas_call x1, Pallas kernels, local(): pl.pallas_call(kernel, out_shape=(jax.ShapeDtypeStruct((1, 64, 128), BF16...  74.2 us

profile of v4, /device:TPU:1, one launch (start us, length us, event | category | flops | bytes accessed | tf_op | source)
XLA Modules:
  0.0 76.7 jit_solution(1594096636175538380)
XLA Ops:
  1.3 74.2 %shard_map.68 = (bf16[1,64,128]{2,1,0:T(8,128)(2,1)S(1)}, f32[64,64]{1,0:T(8,128)S(1)}) custom-call(bf16[1,64,128]{2,1,0:T(8,128)(2,1)} %bitcast.7, bf16[96,128,128]{2,1,0:T(8,128)(2,1)} %bitcast.6, s32[1,96]{1,0:T(1,128)} %bitcast.8, s32[1,96]{1,0:T(1,128)} %bitcast.9, s32[1,1]{1,0:T(1,128)S(6)} %copy.9.count_ref), custom_call_target="tpu_custom_call" | custom-call | tf_op jit(solution)/shard_map/pallas_call | solution.py:255
  75.5 0.6 copy.10
  76.1 0.6 copy.11

commit v5 on v4

--- a/solution.py
+++ b/solution.py
@@ -33,7 +33,7 @@
 def kernel(
     x_ref, tiles_ref, rows_ref, cols_ref, count_ref, filtered_ref, gram_ref,
     tile_buf, rows_buf, cols_buf, lines, table, slab_x0, slab_x1, slab_f0, slab_f1, seg,
-    y_out, y_in, z_out, z_in, first_z, g_send, g_row, g_y, g_z, g_all,
+    y_out, y_in, z_out, z_in, first_z, g_send, g_plane, g_z, g_all,
     in_sem, ag_send, ag_recv, y_send, y_recv, z_send, z_recv, f_send, f_recv, g_ssem, g_rsem,
 ):
     col, row = lax.axis_index("col"), lax.axis_index("row")
@@ -67,7 +67,12 @@
     barrier = pltpu.get_barrier_semaphore()
     z_steps = OFFSETS[:-1]
     row_steps = (4, 5, 3, 2, 6, 7, 1)
-    peers = [at_z(i) for i in z_steps] + [at_y(i) for i in Y_STEPS] + [at_row(i) for i in row_steps]
+    plane_steps = [(s, i) for s in (*Y_STEPS, 0) for i in (*row_steps, 0)][:-1]
+
+    def at_plane(step):
+        return (lax.rem(y + step[0], NY) * NZ + z, lax.rem(row + step[1], NROW))
+
+    peers = [at_z(i) for i in z_steps] + [at_plane(step) for step in plane_steps]
     for peer in peers:
         pl.semaphore_signal(barrier, inc=1, device_id=peer, device_id_type=MESH)
     for p in range(PARTS):
@@ -96,7 +101,7 @@
         waiting(ag_send.at[k, p], ag_recv.at[k, p], slabs[k][p].at[: NROW - 1]).wait_recv()
 
     def products(k, p):
-        group = 32
+        group = 48
 
         def step(i, acc):
             base = i * group
@@ -127,7 +132,7 @@
                 ).start()
         sent.append(waiting(y_send.at[k, p], y_recv.at[k, p, 0], y_out.at[k, p]))
 
-    def z_start(k, p, q):
+    def z_start(k, p, q, held=None):
         offsets = OFFSETS[q * PER : (q + 1) * PER]
         waiting(y_send.at[k, p], y_recv.at[k, p, q], y_in.at[k, p, q]).wait_recv()
         sums = []
@@ -139,7 +144,11 @@
             if offset:
                 at = offset - 1
                 z_out[k, p, at] = encode(total)
-                remote(z_out.at[k, p, at], z_in.at[k, p, at], z_send.at[k, p], z_recv.at[k, p], at_z(offset)).start()
+                c = remote(z_out.at[k, p, at], z_in.at[k, p, at], z_send.at[k, p], z_recv.at[k, p], at_z(offset))
+                if held is None:
+                    c.start()
+                else:
+                    held.append(c)
         if q == CHUNKS - 1:
             sent.append(waiting(z_send.at[k, p], z_recv.at[k, p], z_out.at[k, p]))
         return offsets, sums
@@ -164,24 +173,30 @@
             _, sums = z_start(0, p, q)
         own.append(sums[-1])
 
+    def first_over_z(p):
+        for i in z_steps:
+            remote(slabs[1][p].at[row], first_z.at[p, NZ - i], f_send.at[p], f_recv.at[p], at_z(i)).start()
+        sent.append(waiting(f_send.at[p], f_recv.at[p], first_z.at[p, 1:]))
+
     for p in range(PARTS):
         first = z_wait(0, p, own[p]).astype(BF16)
         slabs[1][p][row] = first
         gather_start(1, p)
         first_z[p, 0] = first
-        for i in z_steps:
-            remote(slabs[1][p].at[row], first_z.at[p, NZ - i], f_send.at[p], f_recv.at[p], at_z(i)).start()
-        sent.append(waiting(f_send.at[p], f_recv.at[p], first_z.at[p, 1:]))
+        if p == 0:
+            first_over_z(p)
     for p in range(PARTS):
         gather_wait(1, p)
         products(1, p)
         y_start(1, p)
-
-    own = []
+        if p == 0:
+            first_over_z(1)
+
+    own, held = [], []
     for p in range(PARTS):
         term = None
         for q in range(CHUNKS):
-            offsets, sums = z_start(1, p, q)
+            offsets, sums = z_start(1, p, q, held if p == PARTS - 1 else None)
             if p == q == 0:
                 for h in range(PARTS):
                     waiting(f_send.at[h], f_recv.at[h], first_z.at[h, 1:]).wait_recv()
@@ -212,11 +227,17 @@
             total = total + buf[i]
         return total
 
-    g_row[row] = g_send[row]
-    spread(g_row, row_steps, NROW, row, at_row, 0, lambda i: g_send.at[lax.rem(row + i, NROW)])()
-    g_y[y] = added(g_row, NROW)
-    spread(g_y, Y_STEPS, NY, y, at_y, 1)()
-    g_z[z] = added(g_y, NY)
+    mine = y * NROW + row
+    g_plane[mine] = g_send[row]
+    for step in plane_steps:
+        src = g_send.at[lax.rem(row + step[1], NROW)]
+        remote(src, g_plane.at[mine], g_ssem.at[0], g_rsem.at[0], at_plane(step)).start()
+    plane = waiting(g_ssem.at[0], g_rsem.at[0], g_plane.at[: NY * NROW - 1])
+    sent.append(plane)
+    for c in held:
+        c.start()
+    plane.wait_recv()
+    g_z[z] = added(g_plane, NY * NROW)
     g_wait = spread(g_z, z_steps, NZ, z, at_z, 2)
     for p in range(PARTS):
         filtered_ref[0, p * WIDE : (p + 1) * WIDE, :] = z_wait(1, p, own[p]).astype(BF16)
@@ -271,8 +292,7 @@
             pltpu.VMEM((2, PARTS, NZ - 1, WIDE, 128), BF16),
             pltpu.VMEM((PARTS, NZ, WIDE, 128), BF16),
             pltpu.VMEM((NROW, 8, 64), F32),
-            pltpu.VMEM((NROW, 8, 64), F32),
-            pltpu.VMEM((NY, 8, 64), F32),
+            pltpu.VMEM((NY * NROW, 8, 64), F32),
             pltpu.VMEM((NZ, 8, 64), F32),
             pltpu.VMEM((NROW, 8, 64), F32),
             dma((7,)),

time: 76.8 us -> 74.8 us (0.974)
  Pallas kernels: 74.2 us -> 72 us
    pallas_call x1, Pallas kernels: 74.2 us -> 72 us  [local(): pl.pallas_call(kernel, out_shape=(jax.ShapeDtypeStruct((1, 64, 128), BF16...]
where the time goes in v5:
time: 74.8 us; the launch traced here: 74.5 us
  Pallas kernels  72 us (96%)
  between operations  1.29 us (2%)
  local copies, waits for them, and re-layouts  1.22 us (2%)
    pallas_call x1, Pallas kernels, local(): pl.pallas_call(kernel, out_shape=(jax.ShapeDtypeStruct((1, 64, 128), BF16...  72 us

profile of v5, /device:TPU:1, one launch (start us, length us, event | category | flops | bytes accessed | tf_op | source)
XLA Modules:
  0.0 74.5 jit_solution(14842103525262260266)
XLA Ops:
  1.3 72.0 %shard_map.68 = (bf16[1,64,128]{2,1,0:T(8,128)(2,1)S(1)}, f32[64,64]{1,0:T(8,128)S(1)}) custom-call(bf16[1,64,128]{2,1,0:T(8,128)(2,1)} %bitcast.7, bf16[96,128,128]{2,1,0:T(8,128)(2,1)} %bitcast.6, s32[1,96]{1,0:T(1,128)} %bitcast.8, s32[1,96]{1,0:T(1,128)} %bitcast.9, s32[1,1]{1,0:T(1,128)S(6)} %copy.9.count_ref), custom_call_target="tpu_custom_call" | custom-call | tf_op jit(solution)/shard_map/pallas_call | solution.py:276
  73.3 0.6 copy.10
  73.9 0.6 copy.11

commit v6 on v5

--- a/solution.py
+++ b/solution.py
@@ -192,6 +192,21 @@
         if p == 0:
             first_over_z(1)
 
+    mine = y * NROW + row
+    shared = NROW // PARTS
+
+    def plane_start(p):
+        for s in (*Y_STEPS, 0):
+            for j in (2, 1, 3, 0):
+                owner = p * shared + lax.rem(row + j, shared)
+                c = remote(
+                    g_send.at[owner], g_plane.at[mine], g_ssem.at[0], g_rsem.at[0], (lax.rem(y + s, NY) * NZ + z, owner)
+                )
+                if s or j:
+                    c.start()
+                else:
+                    pl.when(lax.div(row, shared) != p)(c.start)
+
     own, held = [], []
     for p in range(PARTS):
         term = None
@@ -212,6 +227,7 @@
         own.append(sums[-1])
         for r in range(NROW // PARTS):
             g_send[p * (NROW // PARTS) + r] = term[8 * r : 8 * r + 8, :]
+        plane_start(p)
 
     def spread(buf, steps, size, mine, device, sem, source=None):
         for i in steps:
@@ -227,11 +243,7 @@
             total = total + buf[i]
         return total
 
-    mine = y * NROW + row
     g_plane[mine] = g_send[row]
-    for step in plane_steps:
-        src = g_send.at[lax.rem(row + step[1], NROW)]
-        remote(src, g_plane.at[mine], g_ssem.at[0], g_rsem.at[0], at_plane(step)).start()
     plane = waiting(g_ssem.at[0], g_rsem.at[0], g_plane.at[: NY * NROW - 1])
     sent.append(plane)
     for c in held:

time: 74.8 us -> 75.4 us (level)
  no operation moved by 1% of the time
where the time goes in v6:
time: 75.4 us; the launch traced here: 75.2 us
  Pallas kernels  72.7 us (96%)
  between operations  1.29 us (2%)
  local copies, waits for them, and re-layouts  1.22 us (2%)
    pallas_call x1, Pallas kernels, local(): pl.pallas_call(kernel, out_shape=(jax.ShapeDtypeStruct((1, 64, 128), BF16...  72.7 us

profile of v6, /device:TPU:1, one launch (start us, length us, event | category | flops | bytes accessed | tf_op | source)
XLA Modules:
  0.0 75.2 jit_solution(13680376979603498971)
XLA Ops:
  1.3 72.7 %shard_map.68 = (bf16[1,64,128]{2,1,0:T(8,128)(2,1)S(1)}, f32[64,64]{1,0:T(8,128)S(1)}) custom-call(bf16[1,64,128]{2,1,0:T(8,128)(2,1)} %bitcast.7, bf16[96,128,128]{2,1,0:T(8,128)(2,1)} %bitcast.6, s32[1,96]{1,0:T(1,128)} %bitcast.8, s32[1,96]{1,0:T(1,128)} %bitcast.9, s32[1,1]{1,0:T(1,128)S(6)} %copy.9.count_ref), custom_call_target="tpu_custom_call" | custom-call | tf_op jit(solution)/shard_map/pallas_call | solution.py:288
  73.9 0.6 copy.10
  74.6 0.6 copy.11
